TPU v7x, 128 devices: a whole 4x4x4 slice. The times are simulated.
128 devices in a mesh: expert: 32 (over z, y, core), helper: 4 (over x).
Axes of the slice: x: 4, y: 4, z: 4, core: 2. Of those that a mesh axis runs over, the one named last changes fastest.
Arguments:
- tokens: bfloat16 [131072, 768], P(('expert', 'helper')), may hold values from -6 to 6
- gate: float32 [131072], P(('expert', 'helper')), may hold values from 0.2 to 1
- expert_ids: int32 [131072, 1], P(('expert', 'helper')), may hold values from 0 to 127; in each aligned block of 1024 rows (0 to 1023, 1024 to 2047, ...) at most 12 rows name the same one
- backup_ids: int32 [131072, 1], P(('expert', 'helper')), may hold values from 0 to 127; in each aligned block of 1024 rows (0 to 1023, 1024 to 2047, ...) at most 12 rows name the same one
- capacity: int32 [128], replicated, may hold values from 2 to 12
- w_in: bfloat16 [128, 768, 3072], P('expert', None, 'helper'), may hold values from -0.21875 to 0.21875
- w_out: bfloat16 [128, 3072, 768], P('expert', 'helper'), may hold values from -0.109375 to 0.109375
Outputs:
- mixed: bfloat16 [131072, 768], P(('expert', 'helper'))
Inputs may be any that keep to these rules, and one draw needn't show every extreme that they name: `expert_ids`: in the rows of one device no expert is the first expert of more than 12 rows; some expert reaches 12. `backup_ids`: in the rows of one device no expert is the backup of more than 12 rows; some expert reaches 12.
All inputs are finite; a program needn't handle non-finite values.
Results may differ from a plain program's by a relative error of at most 0.0095.
Values may be sent and summed in bfloat16 or wider, within the bound.
No kernel may reach another device: no remote copies, remote signals or barrier semaphores. Data moves between devices by JAX's collectives and lax.ppermute only.
A program may use at most 192 MiB of HBM per device.

v0:
```python
import functools

import jax
import jax.numpy as jnp
from jax import lax
from jax.experimental import pallas as pl
from jax.experimental.pallas import tpu as pltpu
from jax.sharding import Mesh
from jax.sharding import PartitionSpec as P

EXPERT = ("expert_0", "expert_1", "expert_2")
EXPERT_HELPER = ("expert_0", "expert_1", "expert_2", "helper")
CHUNK = 2
BIN = 40
LIST = 960
REACH = 576
CORE_X = ("expert_2", "helper")
NEAR = [(0, 1), (1, 0), (2, 3), (3, 2), (5, 6), (6, 5), (7, 4), (4, 7)]
FAR = [(1, 2), (2, 1), (3, 0), (0, 3), (4, 5), (5, 4), (6, 7), (7, 6)]
F32 = jnp.float32
BF16 = jnp.bfloat16
VMEM_LIMIT = 24 * 1024 * 1024


def dot(a, b):
    return jnp.dot(a, b, preferred_element_type=F32)


def dot_nt(a, b):
    return lax.dot_general(a, b, (((1,), (1,)), ((), ())), preferred_element_type=F32)


def iota(shape, dim):
    return lax.broadcasted_iota(jnp.int32, shape, dim)


def ones_where(cond):
    return jnp.where(cond, 1.0, 0.0).astype(BF16)


def params():
    return pltpu.CompilerParams(vmem_limit_bytes=VMEM_LIMIT)


def cost(flops, read):
    return pl.CostEstimate(flops=flops // 8, bytes_accessed=read // 8, transcendentals=0)


def route_kernel(held, first_ref, backup_ref, cap_ref, gate_ref, row_ref, col_ref, meta_ref):
    count = cap_ref.shape[1]
    toks = first_ref.shape[1]
    chunks = held // CHUNK
    ids = iota((count, toks), 0)
    first = first_ref[...]
    backup = backup_ref[...]
    one = jnp.where(ids == first, 1.0, 0.0)
    two = jnp.where(ids == backup, 1.0, 0.0)
    earlier = ones_where(iota((toks, toks), 0) < iota((toks, toks), 1))
    rank = jnp.sum(dot(one.astype(BF16), earlier) * one, axis=0, keepdims=True)
    cap = jnp.broadcast_to(cap_ref[...].astype(F32), (8, count)).astype(BF16)
    limit = dot(cap, one.astype(BF16))[0:1]
    kept = jnp.where(rank < limit, 1.0, 0.0)
    spill = two * (1.0 - kept)
    spill_rank = jnp.sum(dot(spill.astype(BF16), earlier) * spill, axis=0, keepdims=True)
    mine = one * kept
    n_kept = jnp.sum(mine, axis=1, keepdims=True)
    final = mine + spill
    n_all = jnp.sum(final, axis=1, keepdims=True)
    e0, e1 = iota((count, count), 0), iota((count, count), 1)
    wide = jnp.broadcast_to(n_all, (count, count)).astype(BF16)
    start = dot(ones_where((e1 < e0) & (e1 // CHUNK == e0 // CHUNK)), wide)
    fullest = jnp.max(dot(ones_where(e1 // CHUNK == e0 // CHUNK), wide))
    over = jnp.where(fullest > BIN - 1, 1.0, 0.0)
    for c in range(chunks):
        here = e0 % held // CHUNK == c
        value = jnp.where(e1 == e0 % CHUNK, n_all, jnp.where(e1 == CHUNK, over, 0.0))
        meta_ref[c] = jnp.where(here, value, 0.0).astype(BF16)
    place = jnp.sum(final * start[:, 0:1] + spill * n_kept, axis=0, keepdims=True)
    place = place + jnp.where(kept > 0.5, rank, spill_rank)
    chosen = jnp.where(kept > 0.5, first, backup)
    bins = chosen % held // CHUNK * (count // held) + chosen // held
    row = jnp.where(place < BIN - 1, bins.astype(F32) * BIN + place, -1.0)
    row_ref[...] = jnp.broadcast_to(row, (8, toks)).astype(jnp.int32)
    stacked = jnp.where(
        iota((128, toks), 0) == 0,
        jnp.broadcast_to(row, (128, toks)),
        jnp.broadcast_to(gate_ref[...], (128, toks)),
    )
    col_ref[...] = stacked.T


def route(first, backup, capacity, gate, held):
    toks, count = first.shape[1], capacity.shape[1]
    return pl.pallas_call(
        functools.partial(route_kernel, held),
        out_shape=(
            jax.ShapeDtypeStruct((8, toks), jnp.int32),
            jax.ShapeDtypeStruct((toks, 128), F32),
            jax.ShapeDtypeStruct((held // CHUNK, count, count), BF16),
        ),
        compiler_params=params(),
        cost_estimate=cost(4 * toks * toks * count, toks * 512),
        name="route",
    )(first, backup, capacity, gate)


def dispatch_kernel(chunk, held, row_ref, tok_ref, meta_ref, out_ref):
    rows, toks = out_ref.shape[0], tok_ref.shape[0]
    count = meta_ref.shape[1]
    begin = pl.program_id(0) * rows
    at = iota((rows, toks), 0) + (begin + chunk * (count // held) * BIN)
    value = dot(ones_where(at == row_ref[0:1, :]), tok_ref[...])
    out_ref[...] = value.astype(BF16)
    at = iota((rows, count), 0) + begin
    spare = ones_where((at % BIN == BIN - 1) & (at // BIN == iota((rows, count), 1) // held))
    out_ref[:, 0:count] = (value[:, 0:count] + dot(spare, meta_ref[0])).astype(BF16)


def dispatch(row, tokens, meta, chunk, held):
    toks, wide = tokens.shape
    count = meta.shape[1]
    total = count // held * BIN
    block = total // 2
    return pl.pallas_call(
        functools.partial(dispatch_kernel, chunk, held),
        out_shape=jax.ShapeDtypeStruct((total, wide), BF16),
        grid=(total // block,),
        in_specs=[
            pl.BlockSpec((8, toks), lambda i: (0, 0)),
            pl.BlockSpec((toks, wide), lambda i: (0, 0)),
            pl.BlockSpec((1, count, count), lambda i: (chunk, 0, 0)),
        ],
        out_specs=pl.BlockSpec((block, wide), lambda i: (i, 0)),
        compiler_params=params(),
        cost_estimate=cost(2 * total * toks * wide, 2 * (total + toks) * wide),
        name="dispatch",
    )(row, tokens, meta)


def places_kernel(arrived_ref, row_ref, col_ref, over_ref, top_ref):
    total = arrived_ref.shape[0]
    sources = total // BIN
    spare = ones_where(iota((sources, total), 1) == iota((sources, total), 0) * BIN + (BIN - 1))
    meta = dot(spare, arrived_ref[...]).astype(BF16)
    lane = ones_where(iota((8, 128), 0) == iota((8, 128), 1))
    told = dot_nt(lane, meta)
    n = jnp.where(iota((8, sources), 0) < CHUNK, told, 0.0)
    flagged = jnp.max(jnp.where(iota((8, sources), 0) == CHUNK, told, 0.0))
    each = jnp.sum(n, axis=1, keepdims=True)
    full = (jnp.max(each) > REACH - 1) | (jnp.sum(each) > LIST - 1)
    over = jnp.where((flagged > 0.5) | full, 1.0, 0.0)
    over_ref[...] = jnp.broadcast_to(over, (8, 128))
    top = jnp.broadcast_to(each[0:1], (8, 128))
    high = jnp.floor(top * (1.0 / 128.0))
    lane = iota((8, 128), 1)
    top_ref[...] = jnp.where(lane == 0, high, jnp.where(lane == 1, top - high * 128.0, 0.0))
    base = dot(n.astype(BF16), ones_where(iota((sources, sources), 0) < iota((sources, sources), 1)))
    begin = jnp.zeros((8, sources), F32)
    for j in range(CHUNK):
        ahead = iota((8, sources), 0) > j
        begin = begin + jnp.where(ahead, jnp.broadcast_to(n[j : j + 1], (8, sources)), 0.0)
    shift = base - begin + 128.0
    high = jnp.floor(shift * (1.0 / 128.0))
    low = shift - high * 128.0
    spread = ones_where(iota((sources, total), 1) // BIN == iota((sources, total), 0))
    place = dot(high.astype(BF16), spread) * 128.0 + dot(low.astype(BF16), spread) - 128.0
    begin = dot(begin.astype(BF16), spread)
    end = begin + dot(n.astype(BF16), spread)
    r = (iota((8, total), 1) % BIN).astype(F32)
    place = place + r
    inside = (r >= begin) & (r < end) & (place < REACH - 1) & (r < BIN - 1)
    place = jnp.where(iota((8, total), 0) == 0, place, LIST - 2.0 - place)
    index = jnp.where(inside, place + 1.0, 0.0)
    index = jnp.sum(index, axis=0, keepdims=True) - 1.0
    row_ref[...] = jnp.broadcast_to(index, (8, total)).astype(jnp.int32)
    col_ref[...] = jnp.broadcast_to(index, (128, total)).T


def places(arrived):
    total = arrived.shape[0]
    return pl.pallas_call(
        places_kernel,
        out_shape=(
            jax.ShapeDtypeStruct((8, total), jnp.int32),
            jax.ShapeDtypeStruct((total, 128), F32),
            jax.ShapeDtypeStruct((8, 128), F32),
            jax.ShapeDtypeStruct((8, 128), F32),
        ),
        grid=(1,),
        in_specs=[pl.BlockSpec((total, 128), lambda i: (0, 0))],
        out_specs=(
            pl.BlockSpec((8, total), lambda i: (0, 0)),
            pl.BlockSpec((total, 128), lambda i: (0, 0)),
            pl.BlockSpec((8, 128), lambda i: (0, 0)),
            pl.BlockSpec((8, 128), lambda i: (0, 0)),
        ),
        compiler_params=params(),
        cost_estimate=cost(1 << 25, 1 << 19),
        name="places",
    )(arrived)


def regroup_kernel(index_ref, rows_ref, top_ref, out_ref):
    count, many = out_ref.shape[0], rows_ref.shape[0]
    begin = pl.program_id(0) * count
    here = iota((count, many), 0) + begin
    value = dot(ones_where(here == index_ref[0:1, :]), rows_ref[...])
    out_ref[...] = value.astype(BF16)
    spare = jnp.where(iota((count, 128), 0) + begin == LIST - 1, top_ref[0:1, :], 0.0)
    out_ref[:, 0:128] = (value[:, 0:128] + spare).astype(BF16)


def regroup(index, rows, top):
    many, wide = rows.shape
    block = LIST // 2
    return pl.pallas_call(
        regroup_kernel,
        out_shape=jax.ShapeDtypeStruct((LIST, wide), BF16),
        grid=(LIST // block,),
        in_specs=[
            pl.BlockSpec((8, many), lambda i: (0, 0)),
            pl.BlockSpec((many, wide), lambda i: (0, 0)),
            pl.BlockSpec((8, 128), lambda i: (0, 0)),
        ],
        out_specs=pl.BlockSpec((block, wide), lambda i: (i, 0)),
        compiler_params=params(),
        cost_estimate=cost(2 * LIST * many * wide, 2 * (LIST + many) * wide),
        name="regroup",
    )(index, rows, top)


def weights_kernel(first, in_ref, out_ref, both_ref, sems):
    copies = [
        pltpu.make_async_copy(ref.at[first + i], both_ref.at[k * CHUNK + i], sems.at[k * CHUNK + i])
        for k, ref in enumerate((in_ref, out_ref))
        for i in range(CHUNK)
    ]
    for copy in copies:
        copy.start()
    for copy in copies:
        copy.wait()


def weights(w_in, w_out, first):
    _, wide, hid = w_in.shape
    return pl.pallas_call(
        functools.partial(weights_kernel, first),
        out_shape=jax.ShapeDtypeStruct((2 * CHUNK, wide, hid), w_in.dtype),
        in_specs=[pl.BlockSpec(memory_space=pl.ANY)] * 2,
        out_specs=pl.BlockSpec(memory_space=pl.ANY),
        scratch_shapes=[pltpu.SemaphoreType.DMA((2 * CHUNK,))],
        compiler_params=params(),
        cost_estimate=cost(1, 8 * CHUNK * wide * hid),
        name="weights",
    )(w_in, w_out)


def expert_kernel(rows_ref, in0_ref, out0_ref, in1_ref, out1_ref, part_ref, total_ref):
    step = pl.program_id(0)
    spare = rows_ref[LIST - 16 : LIST, 0:128].astype(F32)
    lane = iota((16, 128), 1)
    scale = jnp.where(lane == 0, 128.0, jnp.where(lane == 1, 1.0, 0.0))
    scale = jnp.where(iota((16, 128), 0) == 15, scale, 0.0)
    top = jnp.sum(spare * scale).astype(jnp.int32)

    def term(begin, in_ref, out_ref):
        at = iota((REACH, 1), 0) + begin
        mine = at < top if begin == 0 else at >= top
        rows = jnp.where(mine, rows_ref[begin : begin + REACH, :], jnp.zeros((), BF16))
        hidden = jnp.maximum(dot(rows, in_ref[0]), 0.0).astype(BF16)
        return dot(hidden, out_ref[0])

    @pl.when(step == 0)
    def _():
        total_ref[REACH:LIST, :] = jnp.zeros((LIST - REACH, total_ref.shape[1]), F32)
        total_ref[0:REACH, :] = term(0, in0_ref, out0_ref)

    @pl.when(step == 1)
    def _():
        total_ref[LIST - REACH : LIST, :] += term(LIST - REACH, in0_ref, out0_ref)

    @pl.when(step == 2)
    def _():
        total_ref[0:REACH, :] += term(0, in1_ref, out1_ref)

    @pl.when(step == 3)
    def _():
        total_ref[LIST - REACH : LIST, :] += term(LIST - REACH, in1_ref, out1_ref)
        part_ref[...] = total_ref[...].astype(part_ref.dtype)


def expert(rows, w_in, w_out, first, other, dtype):
    wide, hid = w_in.shape[1], w_in.shape[2]
    own, theirs = lambda i: jnp.minimum(i, CHUNK - 1), lambda i: jnp.maximum(i - CHUNK, 0)
    whole = pl.BlockSpec((LIST, wide), lambda i: (0, 0))
    return pl.pallas_call(
        expert_kernel,
        out_shape=jax.ShapeDtypeStruct((LIST, wide), dtype),
        grid=(2 * CHUNK,),
        in_specs=[
            whole,
            pl.BlockSpec((1, wide, hid), lambda i: (first + own(i), 0, 0)),
            pl.BlockSpec((1, hid, wide), lambda i: (first + own(i), 0, 0)),
            pl.BlockSpec((1, wide, hid), lambda i: (theirs(i), 0, 0)),
            pl.BlockSpec((1, hid, wide), lambda i: (CHUNK + theirs(i), 0, 0)),
        ],
        out_specs=whole,
        scratch_shapes=[pltpu.VMEM((LIST, wide), F32)],
        compiler_params=pltpu.CompilerParams(vmem_limit_bytes=32 * 1024 * 1024),
        cost_estimate=cost(16 * REACH * wide * hid, 8 * CHUNK * wide * hid + 6 * LIST * wide),
        name="expert",
    )(rows, w_in, w_out, other, other)


def back_kernel(col_ref, own_ref, sent_ref, over_ref, out_ref):
    rows, many = out_ref.shape[0], own_ref.shape[0]
    value = (own_ref[...] + sent_ref[...].astype(F32)).astype(BF16)
    col = col_ref[:, 0:1].astype(jnp.int32)
    result = dot(ones_where(col == iota((rows, many), 1)), value)
    out_ref[...] = result.astype(BF16)
    at = iota((rows, 128), 0) + pl.program_id(0) * rows
    flag = jnp.where(at % BIN == BIN - 1, over_ref[0:1, :], 0.0)
    out_ref[:, 0:128] = (result[:, 0:128] + flag).astype(BF16)


def back(col, own, sent, over):
    total, (many, wide) = col.shape[0], own.shape
    block = total // 2
    whole = pl.BlockSpec((many, wide), lambda i: (0, 0))
    return pl.pallas_call(
        back_kernel,
        out_shape=jax.ShapeDtypeStruct((total, wide), BF16),
        grid=(total // block,),
        in_specs=[
            pl.BlockSpec((block, 128), lambda i: (i, 0)),
            whole,
            whole,
            pl.BlockSpec((8, 128), lambda i: (0, 0)),
        ],
        out_specs=pl.BlockSpec((block, wide), lambda i: (i, 0)),
        compiler_params=params(),
        cost_estimate=cost(2 * total * many * wide, 2 * total * wide + 6 * many * wide),
        name="back",
    )(col, own, sent, over)


def combine_kernel(chunk, last, col_ref, returned_ref, *refs):
    rows, many = refs[-2].shape[0], returned_ref.shape[0]
    col = col_ref[:, 0:1].astype(jnp.int32)
    total = dot(ones_where(col - chunk * many == iota((rows, many), 1)), returned_ref[...])
    if chunk > 0:
        total = total + refs[0][...].astype(F32)
    if last:
        total = total * col_ref[:, 1:2]
    refs[-2][...] = total.astype(BF16)
    spare = iota((many, 128), 0) % BIN == BIN - 1
    over = jnp.max(jnp.where(spare, returned_ref[:, 0:128].astype(F32), 0.0))
    refs[-1][...] = jnp.broadcast_to(over, (8, 128))


def combine(col, returned, chunk, last, so_far):
    toks, (many, wide) = col.shape[0], returned.shape
    block = toks // 2
    extra = [] if so_far is None else [so_far]
    return pl.pallas_call(
        functools.partial(combine_kernel, chunk, last),
        out_shape=(
            jax.ShapeDtypeStruct((toks, wide), BF16),
            jax.ShapeDtypeStruct((8, 128), F32),
        ),
        grid=(toks // block,),
        in_specs=[
            pl.BlockSpec((block, 128), lambda i: (i, 0)),
            pl.BlockSpec((many, wide), lambda i: (0, 0)),
        ]
        + [pl.BlockSpec((block, wide), lambda i: (i, 0))] * len(extra),
        out_specs=(
            pl.BlockSpec((block, wide), lambda i: (i, 0)),
            pl.BlockSpec((8, 128), lambda i: (0, 0)),
        ),
        compiler_params=params(),
        cost_estimate=cost(2 * toks * many * wide, 2 * (many + 2 * toks) * wide),
        name="combine",
    )(col, returned, *extra)


def assign(first, backup, capacity, count, slot):
    columns = jnp.arange(count, dtype=jnp.int32)
    where = jnp.arange(first.shape[0], dtype=jnp.int32)
    earlier = ones_where(where[None, :] < where[:, None])
    onehot = (first[:, None] == columns[None, :]).astype(F32)
    rank = jnp.sum(dot(earlier, onehot.astype(BF16)) * onehot, axis=1)
    limit = jnp.sum(onehot * capacity[None, :].astype(F32), axis=1)
    kept = rank < limit
    spill = jnp.where((backup[:, None] == columns[None, :]) & ~kept[:, None], 1.0, 0.0)
    spill_rank = jnp.sum(dot(earlier, spill.astype(BF16)) * spill, axis=1)
    final = jnp.where(kept, first, backup)
    slots = jnp.where(kept, rank, slot + spill_rank).astype(jnp.int32)
    return slots, final


def general(tokens, gate, first, backup, capacity, w_in, w_out):
    held = w_in.shape[0]
    owners = lax.axis_size(EXPERT)
    helpers = lax.axis_size("helper")
    experts = held * owners
    slot = max(6, 3 * tokens.shape[0] // (2 * experts))
    slots, final = assign(first, backup, capacity, experts, slot)
    wide = tokens.shape[1]
    buffer = jnp.zeros((experts, 2 * slot, wide), BF16).at[final, slots].set(tokens)
    buffer = buffer.reshape(owners, held * 2 * slot, wide)
    arrived = lax.all_to_all(buffer, EXPERT, 0, 0, tiled=True)
    arrived = arrived.reshape(owners, held, 2 * slot, wide)
    rows = [arrived[:, e].reshape(owners * 2 * slot, wide) for e in range(held)]
    totals = [jnp.zeros(r.shape, F32) for r in rows]
    for k in range(helpers):
        turn = [(i, (i + k) % helpers) for i in range(helpers)]
        some_in = lax.ppermute(w_in, "helper", turn) if k else w_in
        some_out = lax.ppermute(w_out, "helper", turn) if k else w_out
        for e in range(held):
            hidden = jnp.maximum(dot(rows[e], some_in[e]), 0.0).astype(BF16)
            totals[e] = totals[e] + dot(hidden, some_out[e]).astype(BF16).astype(F32)
    outputs = [t.astype(BF16).reshape(owners, 2 * slot, wide) for t in totals]
    result = jnp.stack(outputs, axis=1).reshape(owners, held * 2 * slot, wide)
    returned = lax.all_to_all(result, EXPERT, 0, 0, tiled=True)
    picked = returned.reshape(experts, 2 * slot, wide)[final, slots]
    return (gate[:, None] * picked.astype(F32)).astype(BF16)


def after(*values):
    return lax.optimization_barrier(values)


def on_device(tokens, gate, expert_ids, backup_ids, capacity, w_in, w_out):
    held = w_in.shape[0]
    owners = lax.axis_size(EXPERT)
    helpers = lax.axis_size("helper")
    toks, wide = tokens.shape
    chunks = range(held // CHUNK)
    w_parts = [weights(w_in, w_out, c * CHUNK) for c in chunks]
    others = [lax.ppermute(w, CORE_X, NEAR) for w in w_parts]
    row, col, meta = route(
        expert_ids.reshape(1, toks),
        backup_ids.reshape(1, toks),
        capacity.reshape(1, -1),
        gate.reshape(1, toks),
        held,
    )

    def exchange(rows):
        rows = lax.all_to_all(rows.reshape(owners, BIN, wide), EXPERT, 0, 0, tiled=True)
        return rows.reshape(owners * BIN, wide)

    arrived = [exchange(dispatch(row, tokens, meta, c, held)) for c in chunks]
    at_row, at_col, overs, tops = zip(*[places(a) for a in arrived])
    rows = [regroup(at_row[c], arrived[c], tops[c]) for c in chunks]
    theirs = [lax.ppermute(rows[c], CORE_X, FAR) for c in chunks]
    over = functools.reduce(jnp.maximum, overs)
    own, sent = [], []
    for c in chunks:
        k = c * CHUNK
        args = (w_in, w_out, k, others[c])
        sent.append(lax.ppermute(expert(theirs[c], *args, BF16), CORE_X, FAR))
        own.append(expert(rows[c], *args, F32))
    mixed, flags = None, []
    for c in chunks:
        returned = exchange(back(at_col[c], own[c], sent[c], over))
        mixed, flag = combine(col, returned, c, c == chunks[-1], mixed)
        flags.append(flag)
    around = [[(i, (i + k) % helpers) for i in range(helpers)] for k in range(1, helpers)]
    over = functools.reduce(jnp.maximum, [flags[0]] + [lax.ppermute(flags[0], "helper", a) for a in around])
    return lax.cond(
        over[0, 0] > 0.5,
        lambda ops: general(*ops[1:]),
        lambda ops: ops[0],
        (mixed, tokens, gate, expert_ids[:, 0], backup_ids[:, 0], capacity, w_in, w_out),
    )


def solution(mesh):
    torus = Mesh(
        mesh.devices.reshape(4, 4, 2, mesh.shape["helper"]),
        ("expert_0", "expert_1", "expert_2", "helper"),
    )
    in_specs = (
        P(EXPERT_HELPER, None),
        P(EXPERT_HELPER),
        P(EXPERT_HELPER, None),
        P(EXPERT_HELPER, None),
        P(),
        P(EXPERT, None, "helper"),
        P(EXPERT, "helper", None),
    )
    out_specs = P(EXPERT_HELPER, None)
    return jax.shard_map(
        on_device, mesh=torus, in_specs=in_specs, out_specs=out_specs, check_vma=False
    )
```

profile of v0, /device:TPU:0, one launch (start us, length us, event | category | flops | bytes accessed | tf_op | source)
XLA Modules:
  0.0 490.2 jit_solution(8896824002780434844)
XLA Ops:
  0.0 144.1 %weights.2 = bf16[4,768,768]{2,1,0:T(8,128)(2,1)} custom-call(bf16[4,768,768]{2,1,0:T(8,128)(2,1)} %in0_ref.7, bf16[4,768,768]{2,1,0:T(8,128)(2,1)} %out0_ref.7), custom_call_target="tpu_custom_call" | custom-call | bytes 1179648 | tf_op jit(solution)/shard_map/weights/pallas_call | solution.py:246
  144.1 1.7 collective-permute-start.6
  145.8 1.3 route.1
  147.9 2.8 dispatch.2
  152.1 8.8 %all-to-all-start.2 = ((bf16[32,40,768]{2,1,0:T(8,128)(2,1)}), bf16[32,40,768]{2,1,0:T(8,128)(2,1)S(1)}, u32[]{:S(2)}, u32[]{:S(2)}) async-start(bf16[32,40,768]{2,1,0:T(8,128)(2,1)} %bitcast.199), calls=%async_computation.2 | async-start | bytes 3932160 | tf_op jit(solution)/shard_map/all_to_all | solution.py:451
  160.9 144.1 %weights.3 = bf16[4,768,768]{2,1,0:T(8,128)(2,1)} custom-call(bf16[4,768,768]{2,1,0:T(8,128)(2,1)} %in0_ref.7, bf16[4,768,768]{2,1,0:T(8,128)(2,1)} %out0_ref.7), custom_call_target="tpu_custom_call" | custom-call | bytes 1179648 | tf_op jit(solution)/shard_map/weights/pallas_call | solution.py:246
  305.3 2.9 dispatch.3
  310.7 8.3 %all-to-all-start.3 = ((bf16[32,40,768]{2,1,0:T(8,128)(2,1)}), bf16[32,40,768]{2,1,0:T(8,128)(2,1)S(1)}, u32[]{:S(2)}, u32[]{:S(2)}) async-start(bf16[32,40,768]{2,1,0:T(8,128)(2,1)} %bitcast.198), calls=%async_computation.3 | async-start | bytes 3932160 | tf_op jit(solution)/shard_map/all_to_all | solution.py:451
  319.1 1.5 copy-done.1
  321.5 2.3 regroup.2.rows_ref
  323.8 2.1 collective-permute-start.7
  325.9 34.7 %collective-permute-done.7.rows_ref = bf16[960,768]{1,0:T(8,128)(2,1)S(1)} collective-permute-done((bf16[960,768]{1,0:T(8,128)(2,1)S(1)}, bf16[960,768]{1,0:T(8,128)(2,1)S(1)}, u32[]{:S(2)}, u32[]{:S(2)}) %collective-permute-start.7) | collective-permute-done | bytes 1474592 | tf_op jit(solution)/shard_map/ppermute | solution.py:457
  360.6 10.8 %expert.5 = bf16[960,768]{1,0:T(8,128)(2,1)} custom-call(bf16[960,768]{1,0:T(8,128)(2,1)S(1)} %collective-permute-done.7.rows_ref, bf16[4,768,768]{2,1,0:T(8,128)(2,1)} %in0_ref.7, bf16[4,768,768]{2,1,0:T(8,128)(2,1)} %out0_ref.7, bf16[4,768,768]{2,1,0:T(8,128)(2,1)} %collective-permute-done.6.in1_ref.out1_ref, ...), custom_call_target="tpu_custom_call" | custom-call | flops 679477248 | bytes 1732608 | tf_op jit(solution)/shard_map/expert/pallas_call | solution.py:296
  371.4 1.7 collective-permute-start.8
  374.9 3.1 regroup.3.rows_ref
  378.0 2.1 collective-permute-start.13
  380.1 9.8 %expert.4.own_ref = f32[960,768]{1,0:T(8,128)S(1)} custom-call(bf16[960,768]{1,0:T(8,128)(2,1)S(1)} %regroup.2.rows_ref, bf16[4,768,768]{2,1,0:T(8,128)(2,1)} %in0_ref.7, bf16[4,768,768]{2,1,0:T(8,128)(2,1)} %out0_ref.7, bf16[4,768,768]{2,1,0:T(8,128)(2,1)} %collective-permute-done.6.in1_ref.out1_ref, ...), custom_call_target="tpu_custom_call" | custom-call | flops 679477248 | bytes 1732608 | tf_op jit(solution)/shard_map/expert/pallas_call | solution.py:296
  390.0 2.4 collective-permute-done.8.sent_ref
  392.3 4.2 back.2
  397.8 7.6 %all-to-all-start.4 = ((bf16[32,40,768]{2,1,0:T(8,128)(2,1)}), bf16[32,40,768]{2,1,0:T(8,128)(2,1)S(1)}, u32[]{:S(2)}, u32[]{:S(2)}) async-start(bf16[32,40,768]{2,1,0:T(8,128)(2,1)} %bitcast.201), calls=%async_computation.4 | async-start | bytes 3932160 | tf_op jit(solution)/shard_map/all_to_all | solution.py:451
  405.4 2.8 collective-permute-done.13.rows_ref
  408.1 10.6 %expert.7 = bf16[960,768]{1,0:T(8,128)(2,1)S(1)} custom-call(bf16[960,768]{1,0:T(8,128)(2,1)} %collective-permute-done.13.rows_ref, bf16[4,768,768]{2,1,0:T(8,128)(2,1)} %in0_ref.7, bf16[4,768,768]{2,1,0:T(8,128)(2,1)} %out0_ref.7, bf16[4,768,768]{2,1,0:T(8,128)(2,1)} %collective-permute-done.12.in1_ref.out1_ref, ...), custom_call_target="tpu_custom_call" | custom-call | flops 679477248 | bytes 1732608 | tf_op jit(solution)/shard_map/expert/pallas_call | solution.py:296
  418.7 2.0 collective-permute-start.14
  420.7 10.6 %expert.6.own_ref = f32[960,768]{1,0:T(8,128)S(1)} custom-call(bf16[960,768]{1,0:T(8,128)(2,1)} %regroup.3.rows_ref, bf16[4,768,768]{2,1,0:T(8,128)(2,1)} %in0_ref.7, bf16[4,768,768]{2,1,0:T(8,128)(2,1)} %out0_ref.7, bf16[4,768,768]{2,1,0:T(8,128)(2,1)} %collective-permute-done.12.in1_ref.out1_ref, bf16[4,768,768]{2,1,0:T(8,128)(2,1)} %collective-permute-done.12.in1_ref.out1_ref), custom_call_target="tpu_custom_call" | custom-call | flops 679477248 | bytes 1732608 | tf_op jit(solution)/shard_map/expert/pallas_call | solution.py:296
  431.3 8.3 %collective-permute-done.14.sent_ref = bf16[960,768]{1,0:T(8,128)(2,1)S(1)} collective-permute-done((bf16[960,768]{1,0:T(8,128)(2,1)S(1)}, bf16[960,768]{1,0:T(8,128)(2,1)S(1)}, u32[]{:S(2)}, u32[]{:S(2)}) %collective-permute-start.14) | collective-permute-done | bytes 1474592 | tf_op jit(solution)/shard_map/ppermute | solution.py:463
  439.6 2.8 back.3
  443.7 7.7 %all-to-all-start.5 = ((bf16[32,40,768]{2,1,0:T(8,128)(2,1)}), bf16[32,40,768]{2,1,0:T(8,128)(2,1)}, u32[]{:S(2)}, u32[]{:S(2)}) async-start(bf16[32,40,768]{2,1,0:T(8,128)(2,1)} %bitcast.202), calls=%async_computation.5 | async-start | bytes 3932160 | tf_op jit(solution)/shard_map/all_to_all | solution.py:451
  451.4 3.2 combine.2
  455.7 1.7 collective-permute-start.11
  458.3 21.5 %all-to-all-done.5 = bf16[32,40,768]{2,1,0:T(8,128)(2,1)} async-done(((bf16[32,40,768]{2,1,0:T(8,128)(2,1)}), bf16[32,40,768]{2,1,0:T(8,128)(2,1)}, u32[]{:S(2)}, u32[]{:S(2)}) %all-to-all-start.5) | async-done | bytes 1966112 | tf_op jit(solution)/shard_map/all_to_all | solution.py:451
  479.8 1.4 copy-done.9
  481.2 5.3 %combine.3 = (bf16[1024,768]{1,0:T(8,128)(2,1)S(1)}, f32[8,128]{1,0:T(8,128)}) custom-call(f32[1024,128]{1,0:T(8,128)S(1)} %copy-done.7, bf16[1280,768]{1,0:T(8,128)(2,1)} %bitcast.69.returned_ref, bf16[1024,768]{1,0:T(8,128)(2,1)S(1)} %copy-done.9), custom_call_target="tpu_custom_call" | custom-call | flops 251658240 | bytes 638976 | tf_op jit(solution)/shard_map/combine/pallas_call | solution.py:365
  (57 shorter events, 15.0 us)
Async XLA Ops:
  0.0 145.8 %copy-start.18 = (s32[1024,1]{0,1:T(1,128)S(1)}, s32[1024,1]{0,1:T(1,128)}, u32[]{:S(2)}) copy-start(s32[1024,1]{0,1:T(1,128)} %param.11) | copy-start | bytes 12292
  0.0 145.8 %copy-start.20 = (s32[1024,1]{0,1:T(1,128)S(1)}, s32[1024,1]{0,1:T(1,128)}, u32[]{:S(2)}) copy-start(s32[1024,1]{0,1:T(1,128)} %param.12) | copy-start | bytes 12292
  0.0 145.8 %copy-start.24 = (s32[128]{0:T(128)S(1)}, s32[128]{0:T(128)}, u32[]{:S(2)}) copy-start(s32[128]{0:T(128)} %param.13) | copy-start | bytes 1540
  0.0 145.8 %copy-start.19 = (f32[1024]{0:T(1024)S(1)}, f32[1024]{0:T(1024)}, u32[]{:S(2)}) copy-start(f32[1024]{0:T(1024)} %param.10) | copy-start | bytes 12292
  0.0 147.9 %copy-start.14 = (bf16[1024,768]{1,0:T(8,128)(2,1)S(1)}, bf16[1024,768]{1,0:T(8,128)(2,1)}, u32[]{:S(2)}) copy-start(bf16[1024,768]{1,0:T(8,128)(2,1)} %tok_ref.3) | copy-start | bytes 4718596
  144.1 216.5 %collective-permute-start.6 = (bf16[4,768,768]{2,1,0:T(8,128)(2,1)}, bf16[4,768,768]{2,1,0:T(8,128)(2,1)}, u32[]{:S(2)}, u32[]{:S(2)}) collective-permute-start(bf16[4,768,768]{2,1,0:T(8,128)(2,1)} %weights.2), channel_id=1, source_target_pairs={{0,1},{1,0},{2,3},{3,2},{5,6},{6,5},{7,4},{4,7},{8,9},{9,8},{10,11... | collective-permute-start | bytes 14155784 | tf_op jit(solution)/shard_map/ppermute | solution.py:441
  150.8 1.3 copy-start.3
  152.1 157.3 %all-to-all-start.2 = ((bf16[32,40,768]{2,1,0:T(8,128)(2,1)}), bf16[32,40,768]{2,1,0:T(8,128)(2,1)S(1)}, u32[]{:S(2)}, u32[]{:S(2)}) async-start(bf16[32,40,768]{2,1,0:T(8,128)(2,1)} %bitcast.199), calls=%async_computation.2 | async-start | bytes 3932160 | tf_op jit(solution)/shard_map/all_to_all | solution.py:451
  160.9 144.4 %copy-start.15 = (bf16[1024,768]{1,0:T(8,128)(2,1)S(1)}, bf16[1024,768]{1,0:T(8,128)(2,1)}, u32[]{:S(2)}) copy-start(bf16[1024,768]{1,0:T(8,128)(2,1)} %tok_ref.3) | copy-start | bytes 4718596
  305.0 103.2 %collective-permute-start.12 = (bf16[4,768,768]{2,1,0:T(8,128)(2,1)}, bf16[4,768,768]{2,1,0:T(8,128)(2,1)}, u32[]{:S(2)}, u32[]{:S(2)}) collective-permute-start(bf16[4,768,768]{2,1,0:T(8,128)(2,1)} %weights.3), channel_id=1, source_target_pairs={{0,1},{1,0},{2,3},{3,2},{5,6},{6,5},{7,4},{4,7},{8,9},{9,8},{10,11... | collective-permute-start | bytes 14155784 | tf_op jit(solution)/shard_map/ppermute | solution.py:441
  308.1 1.3 copy-start.2
  309.4 1.3 copy-start
  310.7 62.4 %all-to-all-start.3 = ((bf16[32,40,768]{2,1,0:T(8,128)(2,1)}), bf16[32,40,768]{2,1,0:T(8,128)(2,1)S(1)}, u32[]{:S(2)}, u32[]{:S(2)}) async-start(bf16[32,40,768]{2,1,0:T(8,128)(2,1)} %bitcast.198), calls=%async_computation.3 | async-start | bytes 3932160 | tf_op jit(solution)/shard_map/all_to_all | solution.py:451
  319.0 1.5 copy-start.1
  321.5 2.3 copy-start.10
  323.8 36.9 %collective-permute-start.7 = (bf16[960,768]{1,0:T(8,128)(2,1)S(1)}, bf16[960,768]{1,0:T(8,128)(2,1)S(1)}, u32[]{:S(2)}, u32[]{:S(2)}) collective-permute-start(bf16[960,768]{1,0:T(8,128)(2,1)S(1)} %regroup.2.rows_ref), channel_id=1, source_target_pairs={{1,2},{2,1},{3,0},{0,3},{4,5},{5,4},{6,7},{7,6},{9,10},{10,9},{11,... | collective-permute-start | bytes 4423688 | tf_op jit(solution)/shard_map/ppermute | solution.py:457
  371.4 20.9 %collective-permute-start.8 = (bf16[960,768]{1,0:T(8,128)(2,1)}, bf16[960,768]{1,0:T(8,128)(2,1)}, u32[]{:S(2)}, u32[]{:S(2)}) collective-permute-start(bf16[960,768]{1,0:T(8,128)(2,1)} %expert.5), channel_id=1, source_target_pairs={{1,2},{2,1},{3,0},{0,3},{4,5},{5,4},{6,7},{7,6},{9,10},{10,9},{11,... | collective-permute-start | bytes 4423688 | tf_op jit(solution)/shard_map/ppermute | solution.py:463
  378.0 30.1 %collective-permute-start.13 = (bf16[960,768]{1,0:T(8,128)(2,1)}, bf16[960,768]{1,0:T(8,128)(2,1)}, u32[]{:S(2)}, u32[]{:S(2)}) collective-permute-start(bf16[960,768]{1,0:T(8,128)(2,1)} %regroup.3.rows_ref), channel_id=1, source_target_pairs={{1,2},{2,1},{3,0},{0,3},{4,5},{5,4},{6,7},{7,6},{9,10},{10,9},{11,... | collective-permute-start | bytes 4423688 | tf_op jit(solution)/shard_map/ppermute | solution.py:457
  380.1 12.2 %copy-start.11 = (f32[1280,128]{1,0:T(8,128)S(1)}, f32[1280,128]{1,0:T(8,128)}, u32[]{:S(2)}) copy-start(f32[1280,128]{1,0:T(8,128)} %copy-done.10) | copy-start | bytes 1966084
  396.5 1.3 copy-start.4
  397.8 45.9 %all-to-all-start.4 = ((bf16[32,40,768]{2,1,0:T(8,128)(2,1)}), bf16[32,40,768]{2,1,0:T(8,128)(2,1)S(1)}, u32[]{:S(2)}, u32[]{:S(2)}) async-start(bf16[32,40,768]{2,1,0:T(8,128)(2,1)} %bitcast.201), calls=%async_computation.4 | async-start | bytes 3932160 | tf_op jit(solution)/shard_map/all_to_all | solution.py:451
  418.7 20.9 %copy-start.13 = (f32[1280,128]{1,0:T(8,128)S(1)}, f32[1280,128]{1,0:T(8,128)}, u32[]{:S(2)}) copy-start(f32[1280,128]{1,0:T(8,128)} %copy-done.12) | copy-start | bytes 1966084
  418.7 20.9 %collective-permute-start.14 = (bf16[960,768]{1,0:T(8,128)(2,1)S(1)}, bf16[960,768]{1,0:T(8,128)(2,1)S(1)}, u32[]{:S(2)}, u32[]{:S(2)}) collective-permute-start(bf16[960,768]{1,0:T(8,128)(2,1)S(1)} %expert.7), channel_id=1, source_target_pairs={{1,2},{2,1},{3,0},{0,3},{4,5},{5,4},{6,7},{7,6},{9,10},{10,9},{11,... | collective-permute-start | bytes 4423688 | tf_op jit(solution)/shard_map/ppermute | solution.py:463
  442.4 1.3 copy-start.5
  443.7 7.7 %copy-start.7 = (f32[1024,128]{1,0:T(8,128)S(1)}, f32[1024,128]{1,0:T(8,128)}, u32[]{:S(2)}) copy-start(f32[1024,128]{1,0:T(8,128)} %copy-done.6) | copy-start | bytes 1572868
  443.7 36.1 %all-to-all-start.5 = ((bf16[32,40,768]{2,1,0:T(8,128)(2,1)}), bf16[32,40,768]{2,1,0:T(8,128)(2,1)}, u32[]{:S(2)}, u32[]{:S(2)}) async-start(bf16[32,40,768]{2,1,0:T(8,128)(2,1)} %bitcast.202), calls=%async_computation.5 | async-start | bytes 3932160 | tf_op jit(solution)/shard_map/all_to_all | solution.py:451
  454.6 1.1 copy-start.8
  455.7 30.7 %collective-permute-start.10 = (f32[8,128]{1,0:T(8,128)S(1)}, f32[8,128]{1,0:T(8,128)S(1)}, u32[]{:S(2)}, u32[]{:S(2)}) collective-permute-start(f32[8,128]{1,0:T(8,128)S(1)} %get-tuple-element.58), channel_id=1, source_target_pairs={{0,2},{1,3},{2,0},{3,1},{4,6},{5,7},{6,4},{7,5},{8,10},{9,11},{10,... | collective-permute-start | bytes 12296 | tf_op jit(solution)/shard_map/ppermute | solution.py:471
  455.7 30.7 %collective-permute-start.11 = (f32[8,128]{1,0:T(8,128)S(1)}, f32[8,128]{1,0:T(8,128)S(1)}, u32[]{:S(2)}, u32[]{:S(2)}) collective-permute-start(f32[8,128]{1,0:T(8,128)S(1)} %get-tuple-element.58), channel_id=1, source_target_pairs={{0,3},{1,0},{2,1},{3,2},{4,7},{5,4},{6,5},{7,6},{8,11},{9,8},{10,9... | collective-permute-start | bytes 12296 | tf_op jit(solution)/shard_map/ppermute | solution.py:471
  457.5 29.0 %collective-permute-start.9 = (f32[8,128]{1,0:T(8,128)S(1)}, f32[8,128]{1,0:T(8,128)S(1)}, u32[]{:S(2)}, u32[]{:S(2)}) collective-permute-start(f32[8,128]{1,0:T(8,128)S(1)} %get-tuple-element.58), channel_id=1, source_target_pairs={{0,1},{1,2},{2,3},{3,0},{4,5},{5,6},{6,7},{7,4},{8,9},{9,10},{10,1... | collective-permute-start | bytes 12296 | tf_op jit(solution)/shard_map/ppermute | solution.py:471
  479.8 1.4 copy-start.9
  488.8 1.1 copy-start.23
  (2 other events, 1.7 us)
where the time goes:
time: 496 us; the launch traced here: 490 us
  Pallas kernels  360 us (73%)
  waiting for transfers between devices  69.6 us (14%)
  starting transfers between devices  44.8 us (9%)
  local copies, waits for them, and re-layouts  13.9 us (3%)
    pallas_call x2, Pallas kernels, weights(): pl.pallas_call(functools.partial(weights_kernel, first), out_shape=jax.Sh...  288 us
    pallas_call x4, Pallas kernels, expert(): pl.pallas_call(expert_kernel, out_shape=jax.ShapeDtypeStruct((LIST, wide)...  41.8 us
    ppermute x2, waiting for transfers between devices, on_device(): theirs = [lax.ppermute(rows[c], CORE_X, FAR) for c in chunks]  37.5 us
    all_to_all x4, starting transfers between devices, exchange(): lax.all_to_all(rows.reshape(owners, BIN, wide), EXPERT, 0, 0, tiled=True)  32.3 us
    all_to_all x4, waiting for transfers between devices, exchange(): lax.all_to_all(rows.reshape(owners, BIN, wide), EXPERT, 0, 0, tiled=True)  21.5 us
    unnamed x42, local copies, waits for them, and re-layouts  13.4 us
    ppermute x2, waiting for transfers between devices, on_device(): sent.append(lax.ppermute(expert(theirs[c], *args, BF16), CORE_X, FAR))  10.6 us
  transfers between devices with their start and end apart: 13, of which 5 were waited for; matrix products, arithmetic and copies ran while one was open for 0% of the time, Pallas kernels for 44%

commit v1 on v0

--- a/solution.py
+++ b/solution.py
@@ -14,6 +14,8 @@
 BIN = 40
 LIST = 960
 REACH = 576
+WHOLE = ((0, LIST),)
+PARTS = (WHOLE, ((0, 480), (480, 480)))
 CORE_X = ("expert_2", "helper")
 NEAR = [(0, 1), (1, 0), (2, 3), (3, 2), (5, 6), (6, 5), (7, 4), (4, 7)]
 FAR = [(1, 2), (2, 1), (3, 0), (0, 3), (4, 5), (5, 4), (6, 7), (7, 6)]
@@ -43,7 +45,7 @@
 
 
 def cost(flops, read):
-    return pl.CostEstimate(flops=flops // 8, bytes_accessed=read // 8, transcendentals=0)
+    return pl.CostEstimate(flops=flops, bytes_accessed=read, transcendentals=0)
 
 
 def route_kernel(held, first_ref, backup_ref, cap_ref, gate_ref, row_ref, col_ref, meta_ref):
@@ -147,10 +149,10 @@
     n = jnp.where(iota((8, sources), 0) < CHUNK, told, 0.0)
     flagged = jnp.max(jnp.where(iota((8, sources), 0) == CHUNK, told, 0.0))
     each = jnp.sum(n, axis=1, keepdims=True)
-    full = (jnp.max(each) > REACH - 1) | (jnp.sum(each) > LIST - 1)
+    full = (jnp.max(each) > REACH - 1) | (jnp.sum(each) > LIST - 2)
     over = jnp.where((flagged > 0.5) | full, 1.0, 0.0)
     over_ref[...] = jnp.broadcast_to(over, (8, 128))
-    top = jnp.broadcast_to(each[0:1], (8, 128))
+    top = jnp.broadcast_to(each[0:1] + 1.0, (8, 128))
     high = jnp.floor(top * (1.0 / 128.0))
     lane = iota((8, 128), 1)
     top_ref[...] = jnp.where(lane == 0, high, jnp.where(lane == 1, top - high * 128.0, 0.0))
@@ -169,7 +171,7 @@
     r = (iota((8, total), 1) % BIN).astype(F32)
     place = place + r
     inside = (r >= begin) & (r < end) & (place < REACH - 1) & (r < BIN - 1)
-    place = jnp.where(iota((8, total), 0) == 0, place, LIST - 2.0 - place)
+    place = jnp.where(iota((8, total), 0) == 0, place + 1.0, LIST - 2.0 - place)
     index = jnp.where(inside, place + 1.0, 0.0)
     index = jnp.sum(index, axis=0, keepdims=True) - 1.0
     row_ref[...] = jnp.broadcast_to(index, (8, total)).astype(jnp.int32)
@@ -206,17 +208,18 @@
     here = iota((count, many), 0) + begin
     value = dot(ones_where(here == index_ref[0:1, :]), rows_ref[...])
     out_ref[...] = value.astype(BF16)
-    spare = jnp.where(iota((count, 128), 0) + begin == LIST - 1, top_ref[0:1, :], 0.0)
+    at = iota((count, 128), 0) + begin
+    spare = jnp.where((at == 0) | (at == LIST - 1), top_ref[0:1, :], 0.0)
     out_ref[:, 0:128] = (value[:, 0:128] + spare).astype(BF16)
 
 
 def regroup(index, rows, top):
     many, wide = rows.shape
-    block = LIST // 2
+    count, block = LIST, LIST // 2
     return pl.pallas_call(
         regroup_kernel,
-        out_shape=jax.ShapeDtypeStruct((LIST, wide), BF16),
-        grid=(LIST // block,),
+        out_shape=jax.ShapeDtypeStruct((count, wide), BF16),
+        grid=(count // block,),
         in_specs=[
             pl.BlockSpec((8, many), lambda i: (0, 0)),
             pl.BlockSpec((many, wide), lambda i: (0, 0)),
@@ -224,124 +227,147 @@
         ],
         out_specs=pl.BlockSpec((block, wide), lambda i: (i, 0)),
         compiler_params=params(),
-        cost_estimate=cost(2 * LIST * many * wide, 2 * (LIST + many) * wide),
+        cost_estimate=cost(2 * count * many * wide, 2 * (count + many) * wide),
         name="regroup",
     )(index, rows, top)
 
 
-def weights_kernel(first, in_ref, out_ref, both_ref, sems):
-    copies = [
-        pltpu.make_async_copy(ref.at[first + i], both_ref.at[k * CHUNK + i], sems.at[k * CHUNK + i])
-        for k, ref in enumerate((in_ref, out_ref))
-        for i in range(CHUNK)
-    ]
-    for copy in copies:
-        copy.start()
-    for copy in copies:
-        copy.wait()
+def weights_kernel(first, in_ref, out_ref, both_ref, held_ref, read_sems, write_sems):
+    reads, writes = [], []
+    for k, ref in enumerate((in_ref, out_ref)):
+        for i in range(CHUNK):
+            at = k * CHUNK + i
+            reads.append(pltpu.make_async_copy(ref.at[first + i], held_ref.at[at], read_sems.at[at]))
+            writes.append(pltpu.make_async_copy(held_ref.at[at], both_ref.at[at], write_sems.at[at]))
+    for read in reads:
+        read.start()
+    for read, write in zip(reads, writes):
+        read.wait()
+        write.start()
+    for write in writes:
+        write.wait()
 
 
 def weights(w_in, w_out, first):
     _, wide, hid = w_in.shape
+    shape = (2 * CHUNK, wide, hid)
     return pl.pallas_call(
         functools.partial(weights_kernel, first),
-        out_shape=jax.ShapeDtypeStruct((2 * CHUNK, wide, hid), w_in.dtype),
+        out_shape=jax.ShapeDtypeStruct(shape, w_in.dtype),
         in_specs=[pl.BlockSpec(memory_space=pl.ANY)] * 2,
         out_specs=pl.BlockSpec(memory_space=pl.ANY),
-        scratch_shapes=[pltpu.SemaphoreType.DMA((2 * CHUNK,))],
+        scratch_shapes=[
+            pltpu.VMEM(shape, w_in.dtype),
+            pltpu.SemaphoreType.DMA((2 * CHUNK,)),
+            pltpu.SemaphoreType.DMA((2 * CHUNK,)),
+        ],
         compiler_params=params(),
         cost_estimate=cost(1, 8 * CHUNK * wide * hid),
         name="weights",
     )(w_in, w_out)
 
 
-def expert_kernel(rows_ref, in0_ref, out0_ref, in1_ref, out1_ref, part_ref, total_ref):
+def expert_kernel(parts, *refs):
+    n = len(parts)
+    rows_refs, weight_refs = refs[:n], refs[n : n + 4]
+    part_refs, total_refs = refs[-2 * n : -n], refs[-n:]
     step = pl.program_id(0)
-    spare = rows_ref[LIST - 16 : LIST, 0:128].astype(F32)
-    lane = iota((16, 128), 1)
+    at = 0 if parts[0][0] == 0 else parts[0][1] - 16
+    lane, line = iota((16, 128), 1), iota((16, 128), 0)
     scale = jnp.where(lane == 0, 128.0, jnp.where(lane == 1, 1.0, 0.0))
-    scale = jnp.where(iota((16, 128), 0) == 15, scale, 0.0)
-    top = jnp.sum(spare * scale).astype(jnp.int32)
-
-    def term(begin, in_ref, out_ref):
-        at = iota((REACH, 1), 0) + begin
-        mine = at < top if begin == 0 else at >= top
-        rows = jnp.where(mine, rows_ref[begin : begin + REACH, :], jnp.zeros((), BF16))
-        hidden = jnp.maximum(dot(rows, in_ref[0]), 0.0).astype(BF16)
-        return dot(hidden, out_ref[0])
-
-    @pl.when(step == 0)
-    def _():
-        total_ref[REACH:LIST, :] = jnp.zeros((LIST - REACH, total_ref.shape[1]), F32)
-        total_ref[0:REACH, :] = term(0, in0_ref, out0_ref)
-
-    @pl.when(step == 1)
-    def _():
-        total_ref[LIST - REACH : LIST, :] += term(LIST - REACH, in0_ref, out0_ref)
-
-    @pl.when(step == 2)
-    def _():
-        total_ref[0:REACH, :] += term(0, in1_ref, out1_ref)
-
-    @pl.when(step == 3)
-    def _():
-        total_ref[LIST - REACH : LIST, :] += term(LIST - REACH, in1_ref, out1_ref)
-        part_ref[...] = total_ref[...].astype(part_ref.dtype)
-
-
-def expert(rows, w_in, w_out, first, other, dtype):
+    scale = jnp.where(line == (0 if at == 0 else 15), scale, 0.0)
+    top = jnp.sum(rows_refs[0][at : at + 16, 0:128].astype(F32) * scale).astype(jnp.int32)
+
+    def add(upper, begins):
+        in0_ref, out0_ref, in1_ref, out1_ref = weight_refs
+        reach = (0, REACH) if upper else (LIST - REACH, LIST)
+        for (first, count), rows_ref, total_ref in zip(parts, rows_refs, total_refs):
+            low, high = max(reach[0] - first, 0), min(reach[1] - first, count)
+            if begins and low > 0:
+                total_ref[0:low, :] = jnp.zeros((low, total_ref.shape[1]), F32)
+            if begins and high < count:
+                total_ref[high:count, :] = jnp.zeros((count - high, total_ref.shape[1]), F32)
+            place = iota((high - low, 1), 0) + (first + low)
+            mine = place < top if upper else place >= top
+            rows = jnp.where(mine, rows_ref[low:high, :], jnp.zeros((), BF16))
+            term = None
+            for in_ref, out_ref in ((in0_ref, out0_ref), (in1_ref, out1_ref)):
+                hidden = jnp.maximum(dot(rows, in_ref[0]), 0.0).astype(BF16)
+                part = dot(hidden, out_ref[0])
+                term = part if term is None else term + part
+            total_ref[low:high, :] = term if begins else total_ref[low:high, :] + term
+
+    for k in range(CHUNK):
+
+        @pl.when(step == k)
+        def _(k=k):
+            add(k == 0, k == 0)
+            if k == CHUNK - 1:
+                for part_ref, total_ref in zip(part_refs, total_refs):
+                    part_ref[...] = total_ref[...].astype(part_ref.dtype)
+
+
+def expert(rows, parts, w_in, w_out, first, other, dtype, later_than=()):
     wide, hid = w_in.shape[1], w_in.shape[2]
-    own, theirs = lambda i: jnp.minimum(i, CHUNK - 1), lambda i: jnp.maximum(i - CHUNK, 0)
-    whole = pl.BlockSpec((LIST, wide), lambda i: (0, 0))
-    return pl.pallas_call(
-        expert_kernel,
-        out_shape=jax.ShapeDtypeStruct((LIST, wide), dtype),
-        grid=(2 * CHUNK,),
-        in_specs=[
-            whole,
-            pl.BlockSpec((1, wide, hid), lambda i: (first + own(i), 0, 0)),
-            pl.BlockSpec((1, hid, wide), lambda i: (first + own(i), 0, 0)),
-            pl.BlockSpec((1, wide, hid), lambda i: (theirs(i), 0, 0)),
-            pl.BlockSpec((1, hid, wide), lambda i: (CHUNK + theirs(i), 0, 0)),
-        ],
-        out_specs=whole,
-        scratch_shapes=[pltpu.VMEM((LIST, wide), F32)],
+    total = sum(count for _, count in parts)
+    wholes = [pl.BlockSpec((count, wide), lambda i: (0, 0)) for _, count in parts]
+    taken = [pl.BlockSpec((c, wide), lambda i, f=f, c=c: (f // c, 0)) for f, c in parts]
+    made = pl.pallas_call(
+        functools.partial(expert_kernel, parts),
+        out_shape=[jax.ShapeDtypeStruct((count, wide), dtype) for _, count in parts],
+        grid=(CHUNK,),
+        in_specs=taken
+        + [
+            pl.BlockSpec((1, wide, hid), lambda i: (first + i, 0, 0)),
+            pl.BlockSpec((1, hid, wide), lambda i: (first + i, 0, 0)),
+            pl.BlockSpec((1, wide, hid), lambda i: (i, 0, 0)),
+            pl.BlockSpec((1, hid, wide), lambda i: (CHUNK + i, 0, 0)),
+        ]
+        + [pl.BlockSpec(memory_space=pl.ANY)] * len(later_than),
+        out_specs=wholes,
+        scratch_shapes=[pltpu.VMEM((count, wide), F32) for _, count in parts],
         compiler_params=pltpu.CompilerParams(vmem_limit_bytes=32 * 1024 * 1024),
-        cost_estimate=cost(16 * REACH * wide * hid, 8 * CHUNK * wide * hid + 6 * LIST * wide),
+        cost_estimate=cost(8 * total * wide * hid, 8 * CHUNK * wide * hid + 6 * total * wide),
         name="expert",
-    )(rows, w_in, w_out, other, other)
-
-
-def back_kernel(col_ref, own_ref, sent_ref, over_ref, out_ref):
-    rows, many = out_ref.shape[0], own_ref.shape[0]
-    value = (own_ref[...] + sent_ref[...].astype(F32)).astype(BF16)
+    )(*[rows] * len(parts), w_in, w_out, other, other, *later_than)
+    return list(made)
+
+
+def back_kernel(parts, col_ref, over_ref, *refs):
+    n, out_ref = len(parts), refs[-1]
+    rows = out_ref.shape[0]
     col = col_ref[:, 0:1].astype(jnp.int32)
-    result = dot(ones_where(col == iota((rows, many), 1)), value)
+    result = None
+    for i, (first, count) in enumerate(parts):
+        value = (refs[i][...] + refs[n + i][...].astype(F32)).astype(BF16)
+        part = dot(ones_where(col - first == iota((rows, count), 1)), value)
+        result = part if result is None else result + part
     out_ref[...] = result.astype(BF16)
     at = iota((rows, 128), 0) + pl.program_id(0) * rows
     flag = jnp.where(at % BIN == BIN - 1, over_ref[0:1, :], 0.0)
     out_ref[:, 0:128] = (result[:, 0:128] + flag).astype(BF16)
 
 
-def back(col, own, sent, over):
-    total, (many, wide) = col.shape[0], own.shape
+def back(col, own, sent, over, parts):
+    total, wide = col.shape[0], own.shape[1]
     block = total // 2
-    whole = pl.BlockSpec((many, wide), lambda i: (0, 0))
-    return pl.pallas_call(
-        back_kernel,
+    wholes = [pl.BlockSpec((count, wide), lambda i: (0, 0)) for _, count in parts]
+    taken = [pl.BlockSpec((c, wide), lambda i, f=f, c=c: (f // c, 0)) for f, c in parts]
+    return pl.pallas_call(
+        functools.partial(back_kernel, parts),
         out_shape=jax.ShapeDtypeStruct((total, wide), BF16),
         grid=(total // block,),
         in_specs=[
             pl.BlockSpec((block, 128), lambda i: (i, 0)),
-            whole,
-            whole,
             pl.BlockSpec((8, 128), lambda i: (0, 0)),
-        ],
+        ]
+        + taken
+        + wholes,
         out_specs=pl.BlockSpec((block, wide), lambda i: (i, 0)),
         compiler_params=params(),
-        cost_estimate=cost(2 * total * many * wide, 2 * total * wide + 6 * many * wide),
+        cost_estimate=cost(2 * total * LIST * wide, 2 * total * wide + 6 * LIST * wide),
         name="back",
-    )(col, own, sent, over)
+    )(col, over, *[own] * len(parts), *sent)
 
 
 def combine_kernel(chunk, last, col_ref, returned_ref, *refs):
@@ -454,27 +480,30 @@
     arrived = [exchange(dispatch(row, tokens, meta, c, held)) for c in chunks]
     at_row, at_col, overs, tops = zip(*[places(a) for a in arrived])
     rows = [regroup(at_row[c], arrived[c], tops[c]) for c in chunks]
-    theirs = [lax.ppermute(rows[c], CORE_X, FAR) for c in chunks]
+    theirs = [lax.ppermute(r, CORE_X, FAR) for r in rows]
     over = functools.reduce(jnp.maximum, overs)
     own, sent = [], []
     for c in chunks:
         k = c * CHUNK
         args = (w_in, w_out, k, others[c])
-        sent.append(lax.ppermute(expert(theirs[c], *args, BF16), CORE_X, FAR))
-        own.append(expert(rows[c], *args, F32))
+        made = [expert(theirs[c], [p], *args, BF16)[0] for p in PARTS[c]]
+        sent.append([lax.ppermute(m, CORE_X, FAR) for m in made])
+        ahead = [rows[c + 1]] if c < chunks[-1] else []
+        own.append(expert(rows[c], WHOLE, *args, F32, ahead)[0])
     mixed, flags = None, []
     for c in chunks:
-        returned = exchange(back(at_col[c], own[c], sent[c], over))
+        returned = exchange(back(at_col[c], own[c], sent[c], over, PARTS[c]))
         mixed, flag = combine(col, returned, c, c == chunks[-1], mixed)
         flags.append(flag)
     around = [[(i, (i + k) % helpers) for i in range(helpers)] for k in range(1, helpers)]
     over = functools.reduce(jnp.maximum, [flags[0]] + [lax.ppermute(flags[0], "helper", a) for a in around])
-    return lax.cond(
-        over[0, 0] > 0.5,
-        lambda ops: general(*ops[1:]),
-        lambda ops: ops[0],
-        (mixed, tokens, gate, expert_ids[:, 0], backup_ids[:, 0], capacity, w_in, w_out),
+    again = (tokens, gate, expert_ids[:, 0], backup_ids[:, 0], capacity, w_in, w_out)
+    _, mixed = lax.while_loop(
+        lambda state: state[0] > 0.5,
+        lambda state: (jnp.zeros_like(state[0]), general(*again)),
+        (over[0, 0], mixed),
     )
+    return mixed
 
 
 def solution(mesh):

time: 496 us -> 246 us (0.50); the launches traced: 490 us -> 245 us
  Pallas kernels: 360 us -> 84.1 us
  waiting for transfers between devices: 69.6 us -> 101 us
  local copies, waits for them, and re-layouts: 13.9 us -> 7.8 us
    pallas_call x2, Pallas kernels: 288 us -> 7.58 us  [weights(): pl.pallas_call(functools.partial(weights_kernel, first), out_shape=jax.Sh...]
    all_to_all x4, waiting for transfers between devices: 21.5 us -> 44.8 us  [exchange(): lax.all_to_all(rows.reshape(owners, BIN, wide), EXPERT, 0, 0, tiled=True)]
    ppermute x4 -> x5, starting transfers between devices: 7.95 us -> 19.1 us  [the longest x3 15.4 us: on_device(): sent.append([lax.ppermute(m, CORE_X, FAR) for m in made])]
    ppermute x4 -> x5, waiting for transfers between devices: 48.1 us -> 55.8 us  [the longest x2 34.8 us: on_device(): theirs = [lax.ppermute(r, CORE_X, FAR) for r in rows]]
    all_to_all x4, starting transfers between devices: 32.3 us -> 26.1 us  [exchange(): lax.all_to_all(rows.reshape(owners, BIN, wide), EXPERT, 0, 0, tiled=True)]
    unnamed x42 -> x40, local copies, waits for them, and re-layouts: 13.4 us -> 7.22 us
    pallas_call x8 -> x9, Pallas kernels: 54.2 us -> 58.9 us  [the longest x5 44.7 us: expert(): pl.pallas_call(functools.partial(expert_kernel, parts), out_shape=[jax.Sh...]
  transfers between devices with their start and end apart: 13 -> 14, of which waited for: 5 -> 6; matrix products, arithmetic and copies ran while one was open for 0% -> 0% of each run, Pallas kernels for 44% -> 33%
where the time goes in v1:
time: 246 us; the launch traced here: 245 us
  waiting for transfers between devices  101 us (41%)
  Pallas kernels  84.1 us (34%)
  starting transfers between devices  49.4 us (20%)
  local copies, waits for them, and re-layouts  7.8 us (3%)
    all_to_all x4, waiting for transfers between devices, exchange(): lax.all_to_all(rows.reshape(owners, BIN, wide), EXPERT, 0, 0, tiled=True)  44.8 us
    pallas_call x5, Pallas kernels, expert(): pl.pallas_call(functools.partial(expert_kernel, parts), out_shape=[jax.Sh...  44.7 us
    ppermute x2, waiting for transfers between devices, on_device(): theirs = [lax.ppermute(r, CORE_X, FAR) for r in rows]  34.8 us
    all_to_all x4, starting transfers between devices, exchange(): lax.all_to_all(rows.reshape(owners, BIN, wide), EXPERT, 0, 0, tiled=True)  26.1 us
    ppermute x3, waiting for transfers between devices, on_device(): sent.append([lax.ppermute(m, CORE_X, FAR) for m in made])  21 us
    ppermute x3, starting transfers between devices, on_device(): sent.append([lax.ppermute(m, CORE_X, FAR) for m in made])  15.4 us
    pallas_call x2, Pallas kernels, combine(): pl.pallas_call(functools.partial(combine_kernel, chunk, last), out_shape=...  8.83 us
    pallas_call x2, Pallas kernels, back(): pl.pallas_call(functools.partial(back_kernel, parts), out_shape=jax.Shape...  8.82 us
  transfers between devices with their start and end apart: 14, of which 6 were waited for; matrix products, arithmetic and copies ran while one was open for 0% of the time, Pallas kernels for 33%

profile of v1, /device:TPU:0, one launch (start us, length us, event | category | flops | bytes accessed | tf_op | source)
XLA Modules:
  0.0 245.4 jit_solution(12792687874436778722)
XLA Ops:
  0.0 3.8 %weights.2 = bf16[4,768,768]{2,1,0:T(8,128)(2,1)} custom-call(bf16[4,768,768]{2,1,0:T(8,128)(2,1)} %refs_1_.9, bf16[4,768,768]{2,1,0:T(8,128)(2,1)} %refs_2_.9), custom_call_target="tpu_custom_call" | custom-call | flops 1 | bytes 9437184 | tf_op jit(solution)/shard_map/weights/pallas_call | solution.py:254
  3.8 1.7 collective-permute-start.6
  5.5 1.3 route.1
  7.7 2.8 %dispatch.2 = bf16[1280,768]{1,0:T(8,128)(2,1)S(1)} custom-call(s32[8,1024]{1,0:T(8,128)S(1)} %get-tuple-element.75.row_ref, bf16[1024,768]{1,0:T(8,128)(2,1)S(1)} %copy-done.17, bf16[2,128,128]{2,1,0:T(8,128)(2,1)S(1)} %get-tuple-element.76.meta_ref), custom_call_target="tpu_custom_call" | custom-call | flops 2013265920 | bytes 3538944 | tf_op jit(solution)/shard_map/dispatch/pallas_call | solution.py:126
  11.8 8.8 %all-to-all-start.2 = ((bf16[32,40,768]{2,1,0:T(8,128)(2,1)}), bf16[32,40,768]{2,1,0:T(8,128)(2,1)S(1)}, u32[]{:S(2)}, u32[]{:S(2)}) async-start(bf16[32,40,768]{2,1,0:T(8,128)(2,1)} %bitcast.201), calls=%async_computation.2 | async-start | bytes 3932160 | tf_op jit(solution)/shard_map/all_to_all | solution.py:477
  20.6 3.8 %weights.3 = bf16[4,768,768]{2,1,0:T(8,128)(2,1)} custom-call(bf16[4,768,768]{2,1,0:T(8,128)(2,1)} %refs_1_.9, bf16[4,768,768]{2,1,0:T(8,128)(2,1)} %refs_2_.9), custom_call_target="tpu_custom_call" | custom-call | flops 1 | bytes 9437184 | tf_op jit(solution)/shard_map/weights/pallas_call | solution.py:254
  24.6 24.3 %all-to-all-done.2 = bf16[32,40,768]{2,1,0:T(8,128)(2,1)S(1)} async-done(((bf16[32,40,768]{2,1,0:T(8,128)(2,1)}), bf16[32,40,768]{2,1,0:T(8,128)(2,1)S(1)}, u32[]{:S(2)}, u32[]{:S(2)}) %all-to-all-start.2) | async-done | bytes 1966112 | tf_op jit(solution)/shard_map/all_to_all | solution.py:477
  50.7 3.1 %regroup.2.refs_0_ = bf16[960,768]{1,0:T(8,128)(2,1)} custom-call(s32[8,1280]{1,0:T(8,128)S(1)} %get-tuple-element.80.index_ref, bf16[1280,768]{1,0:T(8,128)(2,1)S(1)} %bitcast.198, f32[8,128]{1,0:T(8,128)S(1)} %get-tuple-element.81.top_ref), custom_call_target="tpu_custom_call" | custom-call | flops 1887436800 | bytes 3440640 | tf_op jit(solution)/shard_map/regroup/pallas_call | solution.py:219
  53.9 1.7 collective-permute-start.7
  55.5 2.9 %dispatch.3 = bf16[1280,768]{1,0:T(8,128)(2,1)S(1)} custom-call(s32[8,1024]{1,0:T(8,128)S(1)} %get-tuple-element.75.row_ref, bf16[1024,768]{1,0:T(8,128)(2,1)S(1)} %copy-done.18, bf16[2,128,128]{2,1,0:T(8,128)(2,1)S(1)} %get-tuple-element.76.meta_ref), custom_call_target="tpu_custom_call" | custom-call | flops 2013265920 | bytes 3538944 | tf_op jit(solution)/shard_map/dispatch/pallas_call | solution.py:126
  59.7 4.3 %all-to-all-start.3 = ((bf16[32,40,768]{2,1,0:T(8,128)(2,1)}), bf16[32,40,768]{2,1,0:T(8,128)(2,1)S(1)}, u32[]{:S(2)}, u32[]{:S(2)}) async-start(bf16[32,40,768]{2,1,0:T(8,128)(2,1)} %bitcast.200), calls=%async_computation.3 | async-start | bytes 3932160 | tf_op jit(solution)/shard_map/all_to_all | solution.py:477
  64.0 26.5 %collective-permute-done.7.refs_0_ = bf16[960,768]{1,0:T(8,128)(2,1)S(1)} collective-permute-done((bf16[960,768]{1,0:T(8,128)(2,1)}, bf16[960,768]{1,0:T(8,128)(2,1)S(1)}, u32[]{:S(2)}, u32[]{:S(2)}) %collective-permute-start.7) | collective-permute-done | bytes 1474592 | tf_op jit(solution)/shard_map/ppermute | solution.py:483
  90.5 10.8 %expert.6 = bf16[960,768]{1,0:T(8,128)(2,1)} custom-call(bf16[960,768]{1,0:T(8,128)(2,1)S(1)} %collective-permute-done.7.refs_0_, bf16[4,768,768]{2,1,0:T(8,128)(2,1)} %refs_1_.9, bf16[4,768,768]{2,1,0:T(8,128)(2,1)} %refs_2_.9, bf16[4,768,768]{2,1,0:T(8,128)(2,1)} %collective-permute-done.6.refs_3_.refs_4_, ...), custom_call_target="tpu_custom_call" | custom-call | flops 4529848320 | bytes 13860864 | tf_op jit(solution)/shard_map/expert/pallas_call | solution.py:315
  101.3 1.7 collective-permute-start.8
  104.7 2.3 regroup.3.refs_5_.refs_0_
  107.0 2.1 collective-permute-start.13
  109.1 11.3 %expert.5.refs_0_ = f32[960,768]{1,0:T(8,128)S(1)} custom-call(bf16[960,768]{1,0:T(8,128)(2,1)} %regroup.2.refs_0_, bf16[4,768,768]{2,1,0:T(8,128)(2,1)} %refs_1_.9, bf16[4,768,768]{2,1,0:T(8,128)(2,1)} %refs_2_.9, bf16[4,768,768]{2,1,0:T(8,128)(2,1)} %collective-permute-done.6.refs_3_.refs_4_, bf16[4,768,768]{2,1,0:T(8,128)(2,1)} %collective-permute-done.6.refs_3_.refs_4_, ...), custom_call_target="tpu_custom_call" | custom-call | flops 4529848320 | bytes 13860864 | tf_op jit(solution)/shard_map/expert/pallas_call | solution.py:315
  120.3 17.7 %collective-permute-done.8.refs_1_ = bf16[960,768]{1,0:T(8,128)(2,1)} collective-permute-done((bf16[960,768]{1,0:T(8,128)(2,1)}, bf16[960,768]{1,0:T(8,128)(2,1)}, u32[]{:S(2)}, u32[]{:S(2)}) %collective-permute-start.8) | collective-permute-done | bytes 1474592 | tf_op jit(solution)/shard_map/ppermute | solution.py:490
  138.0 5.1 %back.2 = bf16[1280,768]{1,0:T(8,128)(2,1)} custom-call(f32[1280,128]{1,0:T(8,128)S(1)} %copy-done.5, f32[8,128]{1,0:T(8,128)S(1)} %max.60.over_ref, f32[960,768]{1,0:T(8,128)S(1)} %expert.5.refs_0_, bf16[960,768]{1,0:T(8,128)(2,1)} %collective-permute-done.8.refs_1_), custom_call_target="tpu_custom_call" | custom-call | flops 1887436800 | bytes 6389760 | tf_op jit(solution)/shard_map/back/pallas_call | solution.py:356
  143.2 4.7 %all-to-all-start.4 = ((bf16[32,40,768]{2,1,0:T(8,128)(2,1)}), bf16[32,40,768]{2,1,0:T(8,128)(2,1)}, u32[]{:S(2)}, u32[]{:S(2)}) async-start(bf16[32,40,768]{2,1,0:T(8,128)(2,1)} %bitcast.64), calls=%async_computation.4 | async-start | bytes 3932160 | tf_op jit(solution)/shard_map/all_to_all | solution.py:477
  147.9 8.3 %collective-permute-done.13.refs_0_ = bf16[960,768]{1,0:T(8,128)(2,1)S(1)} collective-permute-done((bf16[960,768]{1,0:T(8,128)(2,1)S(1)}, bf16[960,768]{1,0:T(8,128)(2,1)S(1)}, u32[]{:S(2)}, u32[]{:S(2)}) %collective-permute-start.13) | collective-permute-done | bytes 1474592 | tf_op jit(solution)/shard_map/ppermute | solution.py:483
  156.2 6.8 %expert.8 = bf16[480,768]{1,0:T(8,128)(2,1)S(1)} custom-call(bf16[960,768]{1,0:T(8,128)(2,1)S(1)} %collective-permute-done.13.refs_0_, bf16[4,768,768]{2,1,0:T(8,128)(2,1)} %refs_1_.9, bf16[4,768,768]{2,1,0:T(8,128)(2,1)} %refs_2_.9, bf16[4,768,768]{2,1,0:T(8,128)(2,1)} %collective-permute-done.12.refs_3_.refs_4_, ...), custom_call_target="tpu_custom_call" | custom-call | flops 2264924160 | bytes 11649024 | tf_op jit(solution)/shard_map/expert/pallas_call | solution.py:315
  163.0 13.3 %collective-permute-start.14 = (bf16[480,768]{1,0:T(8,128)(2,1)S(1)}, bf16[480,768]{1,0:T(8,128)(2,1)S(1)}, u32[]{:S(2)}, u32[]{:S(2)}) collective-permute-start(bf16[480,768]{1,0:T(8,128)(2,1)S(1)} %expert.8), channel_id=1, source_target_pairs={{1,2},{2,1},{3,0},{0,3},{4,5},{5,4},{6,7},{7,6},{9,10},{10,9},{11,... | collective-permute-start | bytes 2211848 | tf_op jit(solution)/shard_map/ppermute | solution.py:490
  176.4 6.8 %expert.9 = bf16[480,768]{1,0:T(8,128)(2,1)S(1)} custom-call(bf16[960,768]{1,0:T(8,128)(2,1)S(1)} %collective-permute-done.13.refs_0_, bf16[4,768,768]{2,1,0:T(8,128)(2,1)} %refs_1_.9, bf16[4,768,768]{2,1,0:T(8,128)(2,1)} %refs_2_.9, bf16[4,768,768]{2,1,0:T(8,128)(2,1)} %collective-permute-done.12.refs_3_.refs_4_, ...), custom_call_target="tpu_custom_call" | custom-call | flops 2264924160 | bytes 11649024 | tf_op jit(solution)/shard_map/expert/pallas_call | solution.py:315
  183.6 9.0 %expert.7.refs_0_.refs_1_ = f32[960,768]{1,0:T(8,128)S(1)} custom-call(bf16[960,768]{1,0:T(8,128)(2,1)S(1)} %regroup.3.refs_5_.refs_0_, bf16[4,768,768]{2,1,0:T(8,128)(2,1)S(1)} %bitcast.206, bf16[4,768,768]{2,1,0:T(8,128)(2,1)S(1)} %bitcast.208, bf16[4,768,768]{2,1,0:T(8,128)(2,1)} %collective-permute-done.12.refs_3_.refs_4_, ...), custom_call_target="tpu_custom_call" | custom-call | flops 4529848320 | bytes 13860864 | tf_op jit(solution)/shard_map/expert/pallas_call | solution.py:315
  192.7 3.3 %collective-permute-done.15.refs_3_ = bf16[480,768]{1,0:T(8,128)(2,1)S(1)} collective-permute-done((bf16[480,768]{1,0:T(8,128)(2,1)S(1)}, bf16[480,768]{1,0:T(8,128)(2,1)S(1)}, u32[]{:S(2)}, u32[]{:S(2)}) %collective-permute-start.15) | collective-permute-done | bytes 737312 | tf_op jit(solution)/shard_map/ppermute | solution.py:490
  196.0 3.7 %back.3 = bf16[1280,768]{1,0:T(8,128)(2,1)} custom-call(f32[1280,128]{1,0:T(8,128)S(1)} %copy-done.3, f32[8,128]{1,0:T(8,128)S(1)} %max.60.over_ref, f32[960,768]{1,0:T(8,128)S(1)} %expert.7.refs_0_.refs_1_, f32[960,768]{1,0:T(8,128)S(1)} %expert.7.refs_0_.refs_1_, bf16[480,768]{1,0:T(8,128)(2,1)S(1)} %collective-permute-done.14.refs_2_, ...), custom_call_target="tpu_custom_call" | custom-call | flops 1887436800 | bytes 6389760 | tf_op jit(solution)/shard_map/back/pallas_call | solution.py:356
  199.7 8.3 %all-to-all-start.5 = ((bf16[32,40,768]{2,1,0:T(8,128)(2,1)}), bf16[32,40,768]{2,1,0:T(8,128)(2,1)S(1)}, u32[]{:S(2)}, u32[]{:S(2)}) async-start(bf16[32,40,768]{2,1,0:T(8,128)(2,1)} %bitcast.67), calls=%async_computation.5 | async-start | bytes 3932160 | tf_op jit(solution)/shard_map/all_to_all | solution.py:477
  209.1 4.7 %combine.2 = (bf16[1024,768]{1,0:T(8,128)(2,1)S(1)}, f32[8,128]{1,0:T(8,128)S(1)}) custom-call(f32[1024,128]{1,0:T(8,128)S(1)} %copy-done.7, bf16[1280,768]{1,0:T(8,128)(2,1)} %bitcast.65.returned_ref), custom_call_target="tpu_custom_call" | custom-call | flops 2013265920 | bytes 5111808 | tf_op jit(solution)/shard_map/combine/pallas_call | solution.py:391
  216.0 20.5 %all-to-all-done.5 = bf16[32,40,768]{2,1,0:T(8,128)(2,1)S(1)} async-done(((bf16[32,40,768]{2,1,0:T(8,128)(2,1)}), bf16[32,40,768]{2,1,0:T(8,128)(2,1)S(1)}, u32[]{:S(2)}, u32[]{:S(2)}) %all-to-all-start.5) | async-done | bytes 1966112 | tf_op jit(solution)/shard_map/all_to_all | solution.py:477
  237.5 4.1 %combine.3 = (bf16[1024,768]{1,0:T(8,128)(2,1)}, f32[8,128]{1,0:T(8,128)}) custom-call(f32[1024,128]{1,0:T(8,128)S(1)} %copy-done.8, bf16[1280,768]{1,0:T(8,128)(2,1)S(1)} %bitcast.199, bf16[1024,768]{1,0:T(8,128)(2,1)S(1)} %get-tuple-element.86.refs_0_), custom_call_target="tpu_custom_call" | custom-call | flops 2013265920 | bytes 5111808 | tf_op jit(solution)/shard_map/combine/pallas_call | solution.py:391
  242.9 1.4 while.9
  (60 shorter events, 13.2 us)
Async XLA Ops:
  0.0 5.5 %copy-start.11 = (s32[1024,1]{0,1:T(1,128)S(1)}, s32[1024,1]{0,1:T(1,128)}, u32[]{:S(2)}) copy-start(s32[1024,1]{0,1:T(1,128)} %param.11) | copy-start | bytes 12292
  0.0 5.5 %copy-start.14 = (s32[1024,1]{0,1:T(1,128)S(1)}, s32[1024,1]{0,1:T(1,128)}, u32[]{:S(2)}) copy-start(s32[1024,1]{0,1:T(1,128)} %param.12) | copy-start | bytes 12292
  0.0 5.5 %copy-start.19 = (s32[128]{0:T(128)S(1)}, s32[128]{0:T(128)}, u32[]{:S(2)}) copy-start(s32[128]{0:T(128)} %param.13) | copy-start | bytes 1540
  0.0 5.5 %copy-start.12 = (f32[1024]{0:T(1024)S(1)}, f32[1024]{0:T(1024)}, u32[]{:S(2)}) copy-start(f32[1024]{0:T(1024)} %param.10) | copy-start | bytes 12292
  3.8 3.9 %copy-start.17 = (bf16[1024,768]{1,0:T(8,128)(2,1)S(1)}, bf16[1024,768]{1,0:T(8,128)(2,1)}, u32[]{:S(2)}) copy-start(bf16[1024,768]{1,0:T(8,128)(2,1)} %tok_ref.3) | copy-start | bytes 4718596
  3.8 86.7 %collective-permute-start.6 = (bf16[4,768,768]{2,1,0:T(8,128)(2,1)}, bf16[4,768,768]{2,1,0:T(8,128)(2,1)}, u32[]{:S(2)}, u32[]{:S(2)}) collective-permute-start(bf16[4,768,768]{2,1,0:T(8,128)(2,1)} %weights.2), channel_id=1, source_target_pairs={{0,1},{1,0},{2,3},{3,2},{5,6},{6,5},{7,4},{4,7},{8,9},{9,8},{10,11... | collective-permute-start | bytes 14155784 | tf_op jit(solution)/shard_map/ppermute | solution.py:467
  10.5 1.3 copy-start.1
  11.8 37.2 %all-to-all-start.2 = ((bf16[32,40,768]{2,1,0:T(8,128)(2,1)}), bf16[32,40,768]{2,1,0:T(8,128)(2,1)S(1)}, u32[]{:S(2)}, u32[]{:S(2)}) async-start(bf16[32,40,768]{2,1,0:T(8,128)(2,1)} %bitcast.201), calls=%async_computation.2 | async-start | bytes 3932160 | tf_op jit(solution)/shard_map/all_to_all | solution.py:477
  24.3 131.8 %collective-permute-start.12 = (bf16[4,768,768]{2,1,0:T(8,128)(2,1)}, bf16[4,768,768]{2,1,0:T(8,128)(2,1)}, u32[]{:S(2)}, u32[]{:S(2)}) collective-permute-start(bf16[4,768,768]{2,1,0:T(8,128)(2,1)} %weights.3), channel_id=1, source_target_pairs={{0,1},{1,0},{2,3},{3,2},{5,6},{6,5},{7,4},{4,7},{8,9},{9,8},{10,11... | collective-permute-start | bytes 14155784 | tf_op jit(solution)/shard_map/ppermute | solution.py:467
  50.7 4.8 %copy-start.18 = (bf16[1024,768]{1,0:T(8,128)(2,1)S(1)}, bf16[1024,768]{1,0:T(8,128)(2,1)}, u32[]{:S(2)}) copy-start(bf16[1024,768]{1,0:T(8,128)(2,1)} %tok_ref.3) | copy-start | bytes 4718596
  53.9 36.6 %collective-permute-start.7 = (bf16[960,768]{1,0:T(8,128)(2,1)}, bf16[960,768]{1,0:T(8,128)(2,1)S(1)}, u32[]{:S(2)}, u32[]{:S(2)}) collective-permute-start(bf16[960,768]{1,0:T(8,128)(2,1)} %regroup.2.refs_0_), channel_id=1, source_target_pairs={{1,2},{2,1},{3,0},{0,3},{4,5},{5,4},{6,7},{7,6},{9,10},{10,9},{11,... | collective-permute-start | bytes 4423688 | tf_op jit(solution)/shard_map/ppermute | solution.py:483
  58.4 1.3 copy-start
  59.7 43.3 %all-to-all-start.3 = ((bf16[32,40,768]{2,1,0:T(8,128)(2,1)}), bf16[32,40,768]{2,1,0:T(8,128)(2,1)S(1)}, u32[]{:S(2)}, u32[]{:S(2)}) async-start(bf16[32,40,768]{2,1,0:T(8,128)(2,1)} %bitcast.200), calls=%async_computation.3 | async-start | bytes 3932160 | tf_op jit(solution)/shard_map/all_to_all | solution.py:477
  101.3 36.8 %collective-permute-start.8 = (bf16[960,768]{1,0:T(8,128)(2,1)}, bf16[960,768]{1,0:T(8,128)(2,1)}, u32[]{:S(2)}, u32[]{:S(2)}) collective-permute-start(bf16[960,768]{1,0:T(8,128)(2,1)} %expert.6), channel_id=1, source_target_pairs={{1,2},{2,1},{3,0},{0,3},{4,5},{5,4},{6,7},{7,6},{9,10},{10,9},{11,... | collective-permute-start | bytes 4423688 | tf_op jit(solution)/shard_map/ppermute | solution.py:490
  103.8 0.9 copy-start.2
  107.0 49.2 %collective-permute-start.13 = (bf16[960,768]{1,0:T(8,128)(2,1)S(1)}, bf16[960,768]{1,0:T(8,128)(2,1)S(1)}, u32[]{:S(2)}, u32[]{:S(2)}) collective-permute-start(bf16[960,768]{1,0:T(8,128)(2,1)S(1)} %regroup.3.refs_5_.refs_0_), channel_id=1, source_target_pairs={{1,2},{2,1},{3,0},{0,3},{4,5},{5,4},{6,7},{7,6},{9,10},{10,9},{11,... | collective-permute-start | bytes 4423688 | tf_op jit(solution)/shard_map/ppermute | solution.py:483
  109.1 29.0 %copy-start.5 = (f32[1280,128]{1,0:T(8,128)S(1)}, f32[1280,128]{1,0:T(8,128)}, u32[]{:S(2)}) copy-start(f32[1280,128]{1,0:T(8,128)} %copy-done.4) | copy-start | bytes 1966084
  143.2 56.5 %all-to-all-start.4 = ((bf16[32,40,768]{2,1,0:T(8,128)(2,1)}), bf16[32,40,768]{2,1,0:T(8,128)(2,1)}, u32[]{:S(2)}, u32[]{:S(2)}) async-start(bf16[32,40,768]{2,1,0:T(8,128)(2,1)} %bitcast.64), calls=%async_computation.4 | async-start | bytes 3932160 | tf_op jit(solution)/shard_map/all_to_all | solution.py:477
  156.2 27.4 %slice-start = ((s8[4718592]{0:T(1024)(128)(4,1)}), s8[4194304]{0:T(1024)(128)(4,1)S(1)}, s32[]{:S(2)}) async-start(s8[4718592]{0:T(1024)(128)(4,1)} %bitcast.205), calls=%async_computation.6 | async-start | bytes 8388608
  156.2 27.4 %slice-start.2 = ((s8[4718592]{0:T(1024)(128)(4,1)}), s8[4194304]{0:T(1024)(128)(4,1)S(1)}, s32[]{:S(2)}) async-start(s8[4718592]{0:T(1024)(128)(4,1)} %bitcast.207), calls=%async_computation.8 | async-start | bytes 8388608
  163.0 20.6 %slice-start.1 = ((s8[4718592]{0:T(1024)(128)(4,1)}), s8[524288]{0:T(1024)(128)(4,1)S(1)}, s32[]{:S(2)}) async-start(s8[4718592]{0:T(1024)(128)(4,1)} %bitcast.205), calls=%async_computation.7 | async-start | bytes 1048576
  163.0 20.6 %slice-start.3 = ((s8[4718592]{0:T(1024)(128)(4,1)}), s8[524288]{0:T(1024)(128)(4,1)S(1)}, s32[]{:S(2)}) async-start(s8[4718592]{0:T(1024)(128)(4,1)} %bitcast.207), calls=%async_computation.9 | async-start | bytes 1048576
  163.0 29.6 %collective-permute-start.14 = (bf16[480,768]{1,0:T(8,128)(2,1)S(1)}, bf16[480,768]{1,0:T(8,128)(2,1)S(1)}, u32[]{:S(2)}, u32[]{:S(2)}) collective-permute-start(bf16[480,768]{1,0:T(8,128)(2,1)S(1)} %expert.8), channel_id=1, source_target_pairs={{1,2},{2,1},{3,0},{0,3},{4,5},{5,4},{6,7},{7,6},{9,10},{10,9},{11,... | collective-permute-start | bytes 2211848 | tf_op jit(solution)/shard_map/ppermute | solution.py:490
  183.2 12.8 %copy-start.3 = (f32[1280,128]{1,0:T(8,128)S(1)}, f32[1280,128]{1,0:T(8,128)}, u32[]{:S(2)}) copy-start(f32[1280,128]{1,0:T(8,128)} %copy-done.2) | copy-start | bytes 1966084
  183.2 12.8 %collective-permute-start.15 = (bf16[480,768]{1,0:T(8,128)(2,1)S(1)}, bf16[480,768]{1,0:T(8,128)(2,1)S(1)}, u32[]{:S(2)}, u32[]{:S(2)}) collective-permute-start(bf16[480,768]{1,0:T(8,128)(2,1)S(1)} %expert.9), channel_id=1, source_target_pairs={{1,2},{2,1},{3,0},{0,3},{4,5},{5,4},{6,7},{7,6},{9,10},{10,9},{11,... | collective-permute-start | bytes 2211848 | tf_op jit(solution)/shard_map/ppermute | solution.py:490
  199.7 36.8 %all-to-all-start.5 = ((bf16[32,40,768]{2,1,0:T(8,128)(2,1)}), bf16[32,40,768]{2,1,0:T(8,128)(2,1)S(1)}, u32[]{:S(2)}, u32[]{:S(2)}) async-start(bf16[32,40,768]{2,1,0:T(8,128)(2,1)} %bitcast.67), calls=%async_computation.5 | async-start | bytes 3932160 | tf_op jit(solution)/shard_map/all_to_all | solution.py:477
  208.0 1.0 copy-start.7
  213.8 27.8 %collective-permute-start.10 = (f32[8,128]{1,0:T(8,128)S(1)}, f32[8,128]{1,0:T(8,128)}, u32[]{:S(2)}, u32[]{:S(2)}) collective-permute-start(f32[8,128]{1,0:T(8,128)S(1)} %get-tuple-element.84), channel_id=1, source_target_pairs={{0,2},{1,3},{2,0},{3,1},{4,6},{5,7},{6,4},{7,5},{8,10},{9,11},{10,... | collective-permute-start | bytes 12296 | tf_op jit(solution)/shard_map/ppermute | solution.py:499
  213.9 27.7 %collective-permute-start.11 = (f32[8,128]{1,0:T(8,128)S(1)}, f32[8,128]{1,0:T(8,128)}, u32[]{:S(2)}, u32[]{:S(2)}) collective-permute-start(f32[8,128]{1,0:T(8,128)S(1)} %get-tuple-element.84), channel_id=1, source_target_pairs={{0,3},{1,0},{2,1},{3,2},{4,7},{5,4},{6,5},{7,6},{8,11},{9,8},{10,9... | collective-permute-start | bytes 12296 | tf_op jit(solution)/shard_map/ppermute | solution.py:499
  214.9 26.7 %collective-permute-start.9 = (f32[8,128]{1,0:T(8,128)S(1)}, f32[8,128]{1,0:T(8,128)}, u32[]{:S(2)}, u32[]{:S(2)}) collective-permute-start(f32[8,128]{1,0:T(8,128)S(1)} %get-tuple-element.84), channel_id=1, source_target_pairs={{0,1},{1,2},{2,3},{3,0},{4,5},{5,6},{6,7},{7,4},{8,9},{9,10},{10,1... | collective-permute-start | bytes 12296 | tf_op jit(solution)/shard_map/ppermute | solution.py:499
  236.4 1.0 copy-start.8
  237.5 5.4 %copy-start.13 = (f32[1024]{0:T(1024)S(1)}, f32[1024]{0:T(1024)}, u32[]{:S(2)}) copy-start(f32[1024]{0:T(1024)} %param.10) | copy-start | bytes 12292
  (2 other events, 1.7 us)
